TPU v7x, 512 devices: a whole 4x8x8 slice. The times are simulated.
512 devices in a mesh: freq: 16 (over z_lo, x), tm: 32 (over z_hi, y, core).
Axes of the slice: x: 4, y: 8, z: 8 (z_hi: 2, z_lo: 4; z = z_hi * 4 + z_lo), core: 2. Of those that a mesh axis runs over, the one named last changes fastest.
Arguments:
- baseband: bfloat16 [128, 4, 262144], P('freq', None, 'tm'), may hold values from -3 to 3
- chirp_phase: float32 [128, 16384], P('freq'), may hold values from -3.140625 to 3.140625
- phase_bins: int32 [262144], P('tm'), may hold values from 0 to 1023
Outputs:
- profile: float32 [128, 4, 1024], P('freq', None, 'tm')
Inputs may be any that keep to these rules, and one draw needn't show every extreme that they name: `phase_bins`: each time sample's phase bin.
All inputs are finite; a program needn't handle non-finite values.
Results may differ from a plain program's by a relative error of at most 0.0003.
Values may be sent and summed in bfloat16 or wider, within the bound.
A program may use at most 64 MiB of HBM per device.

v0:
```python
import math
import jax
import jax.numpy as jnp
from jax import lax
from jax.sharding import PartitionSpec as P

BINS = 1024


def shifted(block, axis, distance):
    devices = range(lax.axis_size(axis))
    route = [(i - distance, i) for i in devices if i - distance in devices]
    return lax.ppermute(block, axis, route)


def dft_tables(radix_size):
    indices = jnp.arange(radix_size, dtype=jnp.int32)
    product_small = indices[:, None] * indices[None, :] % radix_size
    angles = product_small.astype(jnp.float32) * (2.0 * math.pi / radix_size)
    product_large = indices[:, None] * indices[None, :] % (radix_size * radix_size)
    twists = product_large.astype(jnp.float32) * (2.0 * math.pi / (radix_size * radix_size))
    return (jnp.cos(angles), -jnp.sin(angles), jnp.cos(twists), -jnp.sin(twists))


def left_product(matrix_real, matrix_imag, vector_real, vector_imag):

    def apply(matrix, vector):
        return jnp.einsum("kn,cpsnm->cpskm", matrix, vector, precision=lax.Precision.HIGH)

    return (
        apply(matrix_real, vector_real) - apply(matrix_imag, vector_imag),
        apply(matrix_real, vector_imag) + apply(matrix_imag, vector_real),
    )


def right_product(vector_real, vector_imag, matrix_real, matrix_imag):

    def apply(vector, matrix):
        return jnp.einsum("cpskn,nm->cpskm", vector, matrix, precision=lax.Precision.HIGH)

    return (
        apply(vector_real, matrix_real) - apply(vector_imag, matrix_imag),
        apply(vector_real, matrix_imag) + apply(vector_imag, matrix_real),
    )


def filter_frames(frames, response_real, response_imag, tables):
    four_real, four_imag, twist_real, twist_imag = tables
    channels, _, frame_count, frame_len = frames.shape
    radix_size = four_real.shape[0]
    keep_count = frame_len // 2
    shaped = frames.reshape(channels, 2, 2, frame_count, radix_size, radix_size)
    input_real = shaped[:, :, 0]
    input_imag = shaped[:, :, 1]
    section_real, section_imag = left_product(four_real, four_imag, input_real, input_imag)
    turned_real = section_real * twist_real - section_imag * twist_imag
    turned_imag = section_real * twist_imag + section_imag * twist_real
    spec_real, spec_imag = right_product(turned_real, turned_imag, four_real, four_imag)
    gain_real = response_real[:, None, None]
    gain_imag = response_imag[:, None, None]
    shaped_real = spec_real * gain_real - spec_imag * gain_imag
    shaped_imag = spec_real * gain_imag + spec_imag * gain_real
    back_real, back_imag = right_product(shaped_real, shaped_imag, four_real, -four_imag)
    untwist_real = back_real * twist_real + back_imag * twist_imag
    untwist_imag = back_imag * twist_real - back_real * twist_imag
    wave_real, wave_imag = left_product(four_real, -four_imag, untwist_real, untwist_imag)
    factor = 1.0 / frame_len
    wave_real = wave_real.reshape(channels, 2, frame_count, frame_len)[..., keep_count:] * factor
    wave_imag = wave_imag.reshape(channels, 2, frame_count, frame_len)[..., keep_count:] * factor
    return (wave_real, wave_imag)


def fold_blocks(stokes, phase_bins):
    channels, _, samples = stokes.shape
    width = min(1024, samples)
    count = samples // width
    bin_ids = jnp.arange(BINS, dtype=jnp.int32)

    def add_block(index, total):
        start = index * width
        part_bins = lax.dynamic_slice_in_dim(phase_bins, start, width, 0)
        part_stokes = lax.dynamic_slice_in_dim(stokes, start, width, 2)
        onehot = (part_bins[:, None] == bin_ids[None, :]).astype(jnp.float32)
        return total + jnp.einsum("cjt,tb->cjb", part_stokes, onehot, precision=lax.Precision.HIGH)

    return lax.fori_loop(0, count, add_block, jnp.zeros((channels, 4, BINS), jnp.float32))


def shards(baseband, chirp_phase, phase_bins):
    channels, _, samples = baseband.shape
    frame_len = chirp_phase.shape[1]
    keep_count = frame_len // 2
    radix_size = math.isqrt(frame_len)
    segments = samples // keep_count
    tables = dft_tables(radix_size)
    turned = chirp_phase.reshape(channels, radix_size, radix_size).transpose(0, 2, 1)
    response_real = jnp.cos(turned)
    response_imag = jnp.sin(turned)
    rim_samples = shifted(baseband, "tm", 1)
    extended = jnp.concatenate([rim_samples, baseband], axis=2).astype(jnp.float32)
    blocks = extended.reshape(channels, 4, segments + 1, keep_count)
    frames = jnp.concatenate([blocks[:, :, :-1], blocks[:, :, 1:]], axis=3)
    wave_real, wave_imag = filter_frames(frames, response_real, response_imag, tables)
    first_real = wave_real[:, 0].reshape(channels, samples)
    first_imag = wave_imag[:, 0].reshape(channels, samples)
    second_real = wave_real[:, 1].reshape(channels, samples)
    second_imag = wave_imag[:, 1].reshape(channels, samples)
    power_first = first_real * first_real + first_imag * first_imag
    power_second = second_real * second_real + second_imag * second_imag
    stokes = jnp.stack(
        [
            power_first + power_second,
            power_first - power_second,
            2.0 * (first_real * second_real + first_imag * second_imag),
            2.0 * (first_real * second_imag - first_imag * second_real),
        ],
        axis=1,
    )
    folded = fold_blocks(stokes, phase_bins)
    factor = 1.0 / float(samples * lax.axis_size("tm") // BINS)
    summed = lax.psum(folded, "tm")
    part_width = BINS // lax.axis_size("tm")
    profile_part = lax.dynamic_slice_in_dim(
        summed, lax.axis_index("tm") * part_width, part_width, 2
    )
    return profile_part * factor


def solution(mesh):
    placed = (P("freq", None, "tm"), P("freq", None), P("tm"))
    return jax.shard_map(
        shards, mesh=mesh, in_specs=placed, out_specs=P("freq", None, "tm"), check_vma=False
    )
```

profile of v0, /device:TPU:1, one launch (start us, length us, event | category | flops | bytes accessed | tf_op | source)
XLA Modules:
  0.0 407.9 jit_solution(17535864532734620487)
XLA Ops:
  6.5 0.0 copy-start.1
  6.5 0.0 all-reduce.2.cloned.1.call-start
  6.5 4.7 %collective-permute-start = (bf16[8,4,8192]{2,1,0:T(4,128)(2,1)}, bf16[8,4,8192]{2,1,0:T(4,128)(2,1)S(1)}, u32[]{:S(2)}, u32[]{:S(2)}) collective-permute-start(bf16[8,4,8192]{2,1,0:T(4,128)(2,1)} %param.5), channel_id=1, source_target_pairs={{0,1},{1,2},{2,3},{3,4},{4,5},{5,6},{6,7},{7,8},{8,9},{9,10},{10,1... | collective-permute-start | bytes 1572872 | tf_op jit(solution)/shard_map/ppermute | solution.py:13
  11.3 0.3 sine_negate_fusion
  11.5 0.1 copy.46
  11.6 0.1 copy.47
  11.7 2.8 cosine_bitcast_fusion
  14.5 0.2 copy.50
  14.8 0.2 copy.53
  15.0 2.7 collective-permute-done
  17.7 0.0 copy-done.1
  17.7 0.7 maximum_convert_fusion
  18.3 0.1 fusion.141
  18.5 1.8 pad_maximum_fusion
  20.3 2.9 reshape.302
  23.2 1.1 fusion.21
  24.3 1.1 fusion.22
  25.4 1.1 fusion.14
  26.6 1.1 fusion.13
  27.7 1.2 fusion.19
  28.9 1.2 fusion.17
  30.1 1.2 convolution_subtract_fusion.2
  31.4 1.2 convolution_add_fusion.2
  32.6 0.9 fusion.31
  33.5 0.9 fusion.41
  34.5 1.1 convolution_add_fusion.1
  35.6 0.9 convolution_subtract_fusion.1
  36.6 1.2 fusion.23
  37.7 1.2 fusion.24
  38.9 2.2 fusion.12
  41.1 2.6 copy.56
  43.7 1.1 slice.44
  44.8 1.1 copy_multiply_fusion.1
  45.9 2.2 fusion.11
  48.1 0.0 copy-start
  48.1 1.6 copy.60
  49.7 0.3 copy_multiply_fusion
  50.1 0.0 copy-done
  50.1 0.1 add_bitcast_fusion
  50.2 0.1 pad_maximum_fusion.1
  50.3 16.3 %while.14 = (s32[]{:T(128)}, f32[8,4,1024]{2,0,1:T(8,128)S(1)}, f32[8,4,8192]{2,0,1:T(8,128)S(1)}, s32[8192]{0:T(1024)}, s32[]{:T(128)}, /*index=5*/s32[]{:T(128)}, s32[]{:T(128)}, s32[]{:T(128)}) while((s32[]{:T(128)}, f32[8,4,1024]{2,0,1:T(8,128)S(1)}, f32[8,4,8192]{2,0,1:T(8,128)S(1)}, s32[8192]{0:T(1024)}, s32[]{:T(128)}, ...), condition=%wide.region_1.2_spmd.clone, body=%wide.region_0.1_spmd.clone.sunk | while | flops 202440704 | bytes 405653 | solution.py:86
  50.3 0.7 dynamic_slice.26
  51.0 1.3 fusion.147
  52.4 0.7 dynamic_slice.26
  53.1 1.3 fusion.147
  54.4 0.7 dynamic_slice.26
  55.1 1.3 fusion.147
  56.4 0.7 dynamic_slice.26
  57.1 1.3 fusion.147
  58.5 0.7 dynamic_slice.26
  59.2 1.3 fusion.147
  60.5 0.7 dynamic_slice.26
  61.2 1.3 fusion.147
  62.5 0.7 dynamic_slice.26
  63.2 1.3 fusion.147
  64.6 0.7 dynamic_slice.26
  65.3 1.3 fusion.147
  66.6 0.7 copy.62
  67.3 0.0 all-reduce.2.cloned.1.call-update
  67.4 332.3 %all-reduce.2.cloned.1.call-done = f32[8,4,1024]{2,1,0:T(4,128)} async-done(((f32[8,4,1024]{2,1,0:T(4,128)}), f32[8,4,1024]{2,1,0:T(4,128)}) %all-reduce.2.cloned.1.call-update) | async-done | bytes 131088 | tf_op jit(solution)/shard_map/psum | solution.py:121
  399.7 1.4 dynamic-slice_multiply_fusion
  (2 shorter events, 0.0 us)
Async XLA Ops:
  6.5 11.1 %copy-start.1 = (bf16[8,4,8192]{2,1,0:T(4,128)(2,1)S(1)}, bf16[8,4,8192]{2,1,0:T(4,128)(2,1)}, u32[]{:S(2)}) copy-start(bf16[8,4,8192]{2,1,0:T(4,128)(2,1)} %param.5) | copy-start | bytes 1572868
  6.5 393.1 %all-reduce.2.cloned.1.call-start = ((), (), s32[]{:S(2)}) async-start(), calls=%async_computation | async-start | bytes 262144 | tf_op jit(solution)/shard_map/psum | solution.py:121
  6.5 11.1 %collective-permute-start = (bf16[8,4,8192]{2,1,0:T(4,128)(2,1)}, bf16[8,4,8192]{2,1,0:T(4,128)(2,1)S(1)}, u32[]{:S(2)}, u32[]{:S(2)}) collective-permute-start(bf16[8,4,8192]{2,1,0:T(4,128)(2,1)} %param.5), channel_id=1, source_target_pairs={{0,1},{1,2},{2,3},{3,4},{4,5},{5,6},{6,7},{7,8},{8,9},{9,10},{10,1... | collective-permute-start | bytes 1572872 | tf_op jit(solution)/shard_map/ppermute | solution.py:13
  48.1 2.0 copy-start
Sparse Core Ops, SparseCore 0:
  67.5 332.1 all-reduce.1
where the time goes:
time: 408 us
  waiting for transfers between devices  335 us (82%)
  matrix products  30.5 us (7%)
  local copies, waits for them, and re-layouts  18.1 us (4%)
  between operations  13.6 us (3%)
  other arithmetic  5.86 us (1%)
  starting transfers between devices  4.7 us (1%)
    psum x1, waiting for transfers between devices, shards(): summed = lax.psum(folded, 'tm')  332 us
    dot_general x8, matrix products, apply(): jnp.einsum('kn,cpsnm->cpskm', matrix, vector, precision=lax.Precision.HIGH)  11.1 us
    dot_general x8, matrix products, add_block(): jnp.einsum('cjt,tb->cjb', part_stokes, onehot, precision=lax.Precision.HIGH)  10.5 us
    dot_general x8, matrix products, apply(): jnp.einsum('cpskn,nm->cpskm', vector, matrix, precision=lax.Precision.HIGH)  8.81 us
  transfers between devices with their start and end apart: 2, of which 2 were waited for; matrix products, arithmetic and copies ran while one was open for 1% of the time, Pallas kernels for 0%

commit v1 on v0

--- a/solution.py
+++ b/solution.py
@@ -118,7 +118,7 @@
     )
     folded = fold_blocks(stokes, phase_bins)
     factor = 1.0 / float(samples * lax.axis_size("tm") // BINS)
-    summed = lax.psum(folded, "tm")
+    summed = jnp.sum(jax.lax.all_gather(folded, "tm"), 0)
     part_width = BINS // lax.axis_size("tm")
     profile_part = lax.dynamic_slice_in_dim(
         summed, lax.axis_index("tm") * part_width, part_width, 2

time: 408 us -> 197 us (0.48)
  waiting for transfers between devices: 335 us -> 122 us
    psum x1 -> x0, waiting for transfers between devices: 332 us -> none  [shards(): summed = lax.psum(folded, 'tm')]
    all_gather x0 -> x1, waiting for transfers between devices: none -> 119 us  [shards(): summed = jnp.sum(jax.lax.all_gather(folded, 'tm'), 0)]
  transfers between devices with their start and end apart: 2 -> 2, of which waited for: 2 -> 2; matrix products, arithmetic and copies ran while one was open for 1% -> 2% of each run, Pallas kernels for 0% -> 0%
where the time goes in v1:
time: 197 us; the launch traced here: 196 us
  waiting for transfers between devices  122 us (62%)
  matrix products  30.4 us (15%)
  local copies, waits for them, and re-layouts  18.6 us (9%)
  between operations  13.6 us (7%)
  other arithmetic  6.99 us (4%)
  starting transfers between devices  4.7 us (2%)
    all_gather x1, waiting for transfers between devices, shards(): summed = jnp.sum(jax.lax.all_gather(folded, 'tm'), 0)  119 us
    dot_general x8, matrix products, apply(): jnp.einsum('kn,cpsnm->cpskm', matrix, vector, precision=lax.Precision.HIGH)  11.1 us
    dot_general x8, matrix products, add_block(): jnp.einsum('cjt,tb->cjb', part_stokes, onehot, precision=lax.Precision.HIGH)  10.5 us
    dot_general x8, matrix products, apply(): jnp.einsum('cpskn,nm->cpskm', vector, matrix, precision=lax.Precision.HIGH)  8.81 us
    dynamic_slice x8, local copies, waits for them, and re-layouts, add_block(): part_bins = lax.dynamic_slice_in_dim(phase_bins, start, width, 0)  5.54 us
    ppermute x1, starting transfers between devices, shifted(): return lax.ppermute(block, axis, route)  4.7 us
  transfers between devices with their start and end apart: 2, of which 2 were waited for; matrix products, arithmetic and copies ran while one was open for 2% of the time, Pallas kernels for 0%

profile of v1, /device:TPU:1, one launch (start us, length us, event | category | flops | bytes accessed | tf_op | source)
XLA Modules:
  0.0 196.4 jit_solution(15029913440367421625)
XLA Ops:
  6.5 0.0 copy-start.1
  6.5 0.0 all-gather.3.cloned.1.call-start
  6.5 4.7 %collective-permute-start = (bf16[8,4,8192]{2,1,0:T(4,128)(2,1)}, bf16[8,4,8192]{2,1,0:T(4,128)(2,1)S(1)}, u32[]{:S(2)}, u32[]{:S(2)}) collective-permute-start(bf16[8,4,8192]{2,1,0:T(4,128)(2,1)} %param.5), channel_id=1, source_target_pairs={{0,1},{1,2},{2,3},{3,4},{4,5},{5,6},{6,7},{7,8},{8,9},{9,10},{10,1... | collective-permute-start | bytes 1572872 | tf_op jit(solution)/shard_map/ppermute | solution.py:13
  11.3 0.3 sine_negate_fusion
  11.5 0.1 copy.71
  11.6 0.1 copy.72
  11.7 2.8 %cosine_bitcast_fusion = (f32[8,128,128]{2,0,1:T(8,128)S(1)}, f32[8,128,128]{2,0,1:T(8,128)S(1)}) fusion(f32[8,16384]{1,0:T(8,128)} %param.6), kind=kLoop, calls=%fused_computation.43 | loop fusion | bytes 1572864 | tf_op jit(solution)/shard_map/cos | solution.py:97
  14.5 0.2 copy.75
  14.8 0.2 copy.78
  15.0 2.7 %collective-permute-done = bf16[8,4,8192]{2,1,0:T(4,128)(2,1)S(1)} collective-permute-done((bf16[8,4,8192]{2,1,0:T(4,128)(2,1)}, bf16[8,4,8192]{2,1,0:T(4,128)(2,1)S(1)}, u32[]{:S(2)}, u32[]{:S(2)}) %collective-permute-start) | collective-permute-done | bytes 524320 | tf_op jit(solution)/shard_map/ppermute | solution.py:13
  17.7 0.0 copy-done.1
  17.7 0.7 maximum_convert_fusion
  18.3 0.1 fusion.141
  18.5 1.8 pad_maximum_fusion
  20.3 2.9 %reshape.302 = f32[8,2,2,1,128,128]{5,4,3,2,1,0:T(8,128)S(1)} reshape(f32[8,4,1,16384]{3,1,0,2:T(4,128)} %pad_maximum_fusion) | data formatting | bytes 4194304 | tf_op jit(solution)/shard_map/reshape | solution.py:52
  23.2 1.1 fusion.21
  24.3 1.1 fusion.22
  25.4 1.1 fusion.14
  26.5 1.1 fusion.13
  27.7 1.2 fusion.19
  28.9 1.2 fusion.17
  30.1 1.2 convolution_subtract_fusion.2
  31.4 1.2 convolution_add_fusion.2
  32.6 0.9 fusion.31
  33.5 0.9 fusion.41
  34.4 1.1 convolution_add_fusion.1
  35.6 0.9 convolution_subtract_fusion.1
  36.5 1.2 fusion.23
  37.7 1.2 fusion.24
  38.9 2.2 %fusion.12 = f32[8,2,1,128,128]{3,4,1,0,2:T(8,128)} fusion(f32[8,2,128,128]{3,2,1,0:T(8,128)S(1)} %fusion.23, f32[8,2,128,128]{3,2,1,0:T(8,128)S(1)} %convolution_subtract_fusion.1, f32[8,2,128,128]{3,2,1,0:T(8,128)S(1)} %convolution_add_fusion.1, f32[128,128]{1,0:T(8,128)S(1)} %get-tuple-element.141, f32[128,128]{1,0:T(8,128)S(1)} %get-tuple-element.142), kind=kOutput, calls=%fused_computation.13 | convolution fusion | flops 202604544 | bytes 4325376 | tf_op jit(solution)/shard_map/kn,cpsnm->cpskm/dot_general | solution.py:28
  41.1 2.6 %copy.81 = f32[8,2,1,128,128]{4,3,2,1,0:T(8,128)} copy(f32[8,2,1,128,128]{3,4,1,0,2:T(8,128)} %fusion.12) | data formatting | bytes 2097152 | tf_op jit(solution)/shard_map/sub | solution.py:31
  43.7 1.1 slice.44
  44.7 1.2 copy_multiply_fusion.1
  45.9 2.2 %fusion.11 = f32[8,2,1,128,128]{3,4,1,0,2:T(8,128)} fusion(f32[8,2,128,128]{3,2,1,0:T(8,128)S(1)} %fusion.24, f32[8,2,128,128]{3,2,1,0:T(8,128)S(1)} %convolution_add_fusion.1, f32[8,2,128,128]{3,2,1,0:T(8,128)S(1)} %convolution_subtract_fusion.1, f32[128,128]{1,0:T(8,128)S(1)} %get-tuple-element.141, f32[128,128]{1,0:T(8,128)S(1)} %get-tuple-element.142), kind=kOutput, calls=%fused_computation.11 | convolution fusion | flops 202604544 | bytes 4325376 | tf_op jit(solution)/shard_map/kn,cpsnm->cpskm/dot_general | solution.py:28
  48.0 0.0 copy-start
  48.0 1.6 copy.85
  49.7 0.3 copy_multiply_fusion
  50.1 0.0 copy-done
  50.1 0.1 add_bitcast_fusion
  50.2 0.1 pad_maximum_fusion.1
  50.3 16.3 %while.14 = (s32[]{:T(128)}, f32[8,4,1024]{2,0,1:T(8,128)S(1)}, f32[8,4,8192]{2,0,1:T(8,128)S(1)}, s32[8192]{0:T(1024)}, s32[]{:T(128)}, /*index=5*/s32[]{:T(128)}, s32[]{:T(128)}, s32[]{:T(128)}) while((s32[]{:T(128)}, f32[8,4,1024]{2,0,1:T(8,128)S(1)}, f32[8,4,8192]{2,0,1:T(8,128)S(1)}, s32[8192]{0:T(1024)}, s32[]{:T(128)}, ...), condition=%wide.region_1.2_spmd.clone, body=%wide.region_0.1_spmd.clone.sunk | while | flops 202440704 | bytes 405653 | solution.py:86
  50.3 0.7 dynamic_slice.26
  51.0 1.3 fusion.147
  52.4 0.7 dynamic_slice.26
  53.1 1.3 fusion.147
  54.4 0.7 dynamic_slice.26
  55.1 1.3 fusion.147
  56.4 0.7 dynamic_slice.26
  57.1 1.3 fusion.147
  58.5 0.7 dynamic_slice.26
  59.2 1.3 fusion.147
  60.5 0.7 dynamic_slice.26
  61.2 1.3 fusion.147
  62.5 0.7 dynamic_slice.26
  63.2 1.3 fusion.147
  64.6 0.7 dynamic_slice.26
  65.3 1.3 fusion.147
  66.6 0.0 copy-start.2
  66.6 0.6 copy-done.2
  67.2 0.0 all-gather.3.cloned.1.call-update
  67.3 119.2 %all-gather.3.cloned.1.call-done = f32[256,4,1024]{2,0,1:T(8,128)} async-done(((f32[8,4,1024]{2,0,1:T(8,128)}), f32[256,4,1024]{2,0,1:T(8,128)}) %all-gather.3.cloned.1.call-update) | async-done | bytes 4194320 | tf_op jit(solution)/shard_map/all_gather | solution.py:121
  186.4 2.4 %bitcast_reduce_fusion = f32[8,4,1024]{2,0,1:T(8,128)S(1)} fusion(f32[256,4,1024]{2,0,1:T(8,128)} %all-gather.3.cloned.1.call-done), kind=kLoop, calls=%fused_computation.8 | loop fusion | flops 1015808 | bytes 4325376 | tf_op jit(solution)/shard_map/reduce_sum | solution.py:121
  188.9 0.1 dynamic-slice_multiply_fusion
  188.9 0.6 copy.87
  (2 shorter events, 0.0 us)
Async XLA Ops:
  6.5 11.1 %copy-start.1 = (bf16[8,4,8192]{2,1,0:T(4,128)(2,1)S(1)}, bf16[8,4,8192]{2,1,0:T(4,128)(2,1)}, u32[]{:S(2)}) copy-start(bf16[8,4,8192]{2,1,0:T(4,128)(2,1)} %param.5) | copy-start | bytes 1572868
  6.5 179.9 %all-gather.3.cloned.1.call-start = ((), (), s32[]{:S(2)}) async-start(), calls=%async_computation | async-start | bytes 4325376 | tf_op jit(solution)/shard_map/all_gather | solution.py:121
  6.5 11.1 %collective-permute-start = (bf16[8,4,8192]{2,1,0:T(4,128)(2,1)}, bf16[8,4,8192]{2,1,0:T(4,128)(2,1)S(1)}, u32[]{:S(2)}, u32[]{:S(2)}) collective-permute-start(bf16[8,4,8192]{2,1,0:T(4,128)(2,1)} %param.5), channel_id=1, source_target_pairs={{0,1},{1,2},{2,3},{3,4},{4,5},{5,6},{6,7},{7,8},{8,9},{9,10},{10,1... | collective-permute-start | bytes 1572872 | tf_op jit(solution)/shard_map/ppermute | solution.py:13
  48.0 2.0 %copy-start = (f32[8,2,1,8192]{3,0,2,1:T(8,128)S(1)}, f32[8,2,1,8192]{3,0,2,1:T(8,128)}, u32[]{:S(2)}) copy-start(f32[8,2,1,8192]{3,0,2,1:T(8,128)} %copy_multiply_fusion.1) | copy-start | bytes 1572868
  66.6 0.6 copy-start.2
Sparse Core Ops, SparseCore 0:
  67.4 118.9 all-gather.2
